TPU v7x, 512 devices: a whole 4x8x8 slice. The times are simulated.
512 devices in a mesh: rows: 32 (over x, z), cols: 16 (over y, core).
Axes of the slice: x: 4, y: 8, z: 8, core: 2. Of those that a mesh axis runs over, the one named last changes fastest.
Arguments:
- targets: float32 [3, 65536], P(None, 'rows'), may hold values from 0 to 1
- sources: float32 [3, 65536], P(None, 'cols'), may hold values from 0 to 1
- weights: float32 [65536], P('cols'), may hold values from 0.5 to 2
- counts: int32 [4096], P('cols'), may hold values from 8 to 16, as said below
- omega: bfloat16 [65536, 128], P('cols'), may hold values from -0.0234375 to 0.0234375
Outputs:
- basis: float32 [65536, 128], P('rows')
- projected: float32 [65536, 128], P(('cols', 'rows'))
Inputs may be any that keep to these rules, and one draw needn't show every extreme that they name: `counts`: some panel uses all 16 nodes.
All inputs are finite; a program needn't handle non-finite values.
Results may differ from a plain program's by a relative error of at most 0.0033.
Values may be sent and summed in bfloat16 or wider, within the bound.
No kernel may reach another device: no remote copies, remote signals or barrier semaphores. Data moves between devices by JAX's collectives and lax.ppermute only.
A program may use at most 64 MiB of HBM per device.

v0:
```python
import math
import jax
import jax.numpy as jnp
from jax import lax
from jax.sharding import PartitionSpec as P

wave_number = 160.0
separation = 2.0


def kernel_cols(targets, src_block, wts_block):
    diff_x = targets[0][None, :] - (src_block[0][:, None] + separation)
    diff_y = targets[1][None, :] - src_block[1][:, None]
    diff_z = targets[2][None, :] - src_block[2][:, None]
    distance = jnp.sqrt(diff_x * diff_x + diff_y * diff_y + diff_z * diff_z)
    return (wts_block[:, None] * jnp.cos(wave_number * distance) / distance).astype(jnp.bfloat16)


def contract_first(left, right):
    return lax.dot_general(
        left, right, (((0,), (0,)), ((), ())), preferred_element_type=jnp.float32
    )


def gram_of(rows_block):
    return jnp.dot(
        rows_block.T,
        rows_block,
        precision=lax.Precision.HIGHEST,
        preferred_element_type=jnp.float32,
    )


def solve_rows(rows_block, gram_matrix):
    lower_factor = jnp.linalg.cholesky(gram_matrix)
    return lax.linalg.triangular_solve(
        lower_factor, rows_block, left_side=False, lower=True, transpose_a=True
    )


def shards(targets, sources, weights, counts, omega):
    rows_here = targets.shape[1]
    cols_here = sources.shape[1]
    rank = omega.shape[1]
    panel_count = counts.shape[0]
    panel_size = cols_here // panel_count
    usable = (
        (lax.broadcasted_iota(jnp.int32, (panel_count, panel_size), 1) < counts[:, None])
        .reshape(-1)
        .astype(jnp.float32)
    )
    node_weight = weights * usable
    block_width = math.gcd(cols_here, 512)
    nblocks = cols_here // block_width
    src_blocks = sources.reshape(3, nblocks, block_width).transpose(1, 0, 2)
    wts_blocks = node_weight.reshape(nblocks, block_width)
    omega_blocks = omega.reshape(nblocks, block_width, rank)

    def sketch_turn(total, inputs):
        kernel_tile = kernel_cols(targets, inputs[0], inputs[1])
        return (total + contract_first(kernel_tile, inputs[2]), None)

    partial_sketch, _ = lax.scan(
        sketch_turn,
        jnp.zeros((rows_here, rank), jnp.float32),
        (src_blocks, wts_blocks, omega_blocks),
    )
    sketch = lax.psum(partial_sketch, "cols")
    gram_matrix = lax.psum(gram_of(sketch), "rows")
    ortho = solve_rows(sketch, gram_matrix)
    ortho_low = ortho.astype(jnp.bfloat16)
    row_devices = lax.axis_size("rows")
    own_count = cols_here // row_devices
    inner_width = math.gcd(lax.axis_size("rows") * own_count, 512)
    inner_blocks = lax.axis_size("rows") * own_count // inner_width
    sub_src_blocks = sources.reshape(3, inner_blocks, inner_width).transpose(1, 0, 2)
    sub_wts_blocks = node_weight.reshape(inner_blocks, inner_width)

    def project_block(inputs):
        kernel_tile = kernel_cols(targets, inputs[0], inputs[1])
        return jnp.dot(kernel_tile, ortho_low, preferred_element_type=jnp.float32)

    projected = lax.psum_scatter(
        lax.map(project_block, (sub_src_blocks, sub_wts_blocks)).reshape(
            lax.axis_size("rows") * own_count, rank
        ),
        "rows",
        scatter_dimension=0,
        tiled=True,
    )
    scaled = ortho * math.sqrt(rows_here * row_devices)
    return (scaled, projected)


def solution(mesh):
    return jax.shard_map(
        shards,
        mesh=mesh,
        in_specs=(P(None, "rows"), P(None, "cols"), P("cols"), P("cols"), P("cols", None)),
        out_specs=(P("rows", None), P(("cols", "rows"), None)),
        check_vma=False,
    )
```

profile of v0, /device:TPU:8, one launch (start us, length us, event | category | flops | bytes accessed | tf_op | source)
XLA Modules:
  0.0 845.4 jit_solution(1076110894502836828)
XLA Ops:
  8.9 154.4 %while.22 = (s32[]{:T(128)}, f32[2048,128]{1,0:T(8,128)S(1)}, f32[8,512]{1,0:T(8,128)S(1)}, f32[3,2048]{1,0:T(4,128)}, f32[8,3,512]{2,1,0:T(4,128)}, /*index=5*/...) while((s32[]{:T(128)}, f32[2048,128]{1,0:T(8,128)S(1)}, f32[8,512]{1,0:T(8,128)S(1)}, ...), condition=%wide.region_1.2_spmd.clone, body=%wide.region_0.1_spmd.clone.sunk | while | flops 281543168 | bytes 2327191 | solution.py:63
  10.6 17.5 %convolution_add_fusion.2 = f32[2048,128]{1,0:T(8,128)S(1)} fusion(f32[512]{0:T(512)S(1)} %bitcast.85, f32[2048]{0:T(1024)S(1)} %bitcast.77, f32[512]{0:T(512)S(1)} %bitcast.84, f32[2048]{0:T(1024)S(1)} %bitcast.78, f32[512]{0:T(512)S(1)} %bitcast.83, f32[2048]{0:T(1024)S(1)} %bitcast.76, f32[512]{0:T(512)S(1)} %bitcast.89, ...), kind=kOutput, calls=%fused_computation.10.clone.1 | convolution fusion | flops 281542656 | bytes 2261505 | tf_op jit(solution)/shard_map/while/body/eval_jaxpr/dot_general | solution.py:20
  29.9 17.5 %convolution_add_fusion.2 = f32[2048,128]{1,0:T(8,128)S(1)} fusion(f32[512]{0:T(512)S(1)} %bitcast.85, f32[2048]{0:T(1024)S(1)} %bitcast.77, f32[512]{0:T(512)S(1)} %bitcast.84, f32[2048]{0:T(1024)S(1)} %bitcast.78, f32[512]{0:T(512)S(1)} %bitcast.83, f32[2048]{0:T(1024)S(1)} %bitcast.76, f32[512]{0:T(512)S(1)} %bitcast.89, ...), kind=kOutput, calls=%fused_computation.10.clone.1 | convolution fusion | flops 281542656 | bytes 2261505 | tf_op jit(solution)/shard_map/while/body/eval_jaxpr/dot_general | solution.py:20
  49.1 17.5 %convolution_add_fusion.2 = f32[2048,128]{1,0:T(8,128)S(1)} fusion(f32[512]{0:T(512)S(1)} %bitcast.85, f32[2048]{0:T(1024)S(1)} %bitcast.77, f32[512]{0:T(512)S(1)} %bitcast.84, f32[2048]{0:T(1024)S(1)} %bitcast.78, f32[512]{0:T(512)S(1)} %bitcast.83, f32[2048]{0:T(1024)S(1)} %bitcast.76, f32[512]{0:T(512)S(1)} %bitcast.89, ...), kind=kOutput, calls=%fused_computation.10.clone.1 | convolution fusion | flops 281542656 | bytes 2261505 | tf_op jit(solution)/shard_map/while/body/eval_jaxpr/dot_general | solution.py:20
  68.4 17.5 %convolution_add_fusion.2 = f32[2048,128]{1,0:T(8,128)S(1)} fusion(f32[512]{0:T(512)S(1)} %bitcast.85, f32[2048]{0:T(1024)S(1)} %bitcast.77, f32[512]{0:T(512)S(1)} %bitcast.84, f32[2048]{0:T(1024)S(1)} %bitcast.78, f32[512]{0:T(512)S(1)} %bitcast.83, f32[2048]{0:T(1024)S(1)} %bitcast.76, f32[512]{0:T(512)S(1)} %bitcast.89, ...), kind=kOutput, calls=%fused_computation.10.clone.1 | convolution fusion | flops 281542656 | bytes 2261505 | tf_op jit(solution)/shard_map/while/body/eval_jaxpr/dot_general | solution.py:20
  87.7 17.5 %convolution_add_fusion.2 = f32[2048,128]{1,0:T(8,128)S(1)} fusion(f32[512]{0:T(512)S(1)} %bitcast.85, f32[2048]{0:T(1024)S(1)} %bitcast.77, f32[512]{0:T(512)S(1)} %bitcast.84, f32[2048]{0:T(1024)S(1)} %bitcast.78, f32[512]{0:T(512)S(1)} %bitcast.83, f32[2048]{0:T(1024)S(1)} %bitcast.76, f32[512]{0:T(512)S(1)} %bitcast.89, ...), kind=kOutput, calls=%fused_computation.10.clone.1 | convolution fusion | flops 281542656 | bytes 2261505 | tf_op jit(solution)/shard_map/while/body/eval_jaxpr/dot_general | solution.py:20
  107.0 17.5 %convolution_add_fusion.2 = f32[2048,128]{1,0:T(8,128)S(1)} fusion(f32[512]{0:T(512)S(1)} %bitcast.85, f32[2048]{0:T(1024)S(1)} %bitcast.77, f32[512]{0:T(512)S(1)} %bitcast.84, f32[2048]{0:T(1024)S(1)} %bitcast.78, f32[512]{0:T(512)S(1)} %bitcast.83, f32[2048]{0:T(1024)S(1)} %bitcast.76, f32[512]{0:T(512)S(1)} %bitcast.89, ...), kind=kOutput, calls=%fused_computation.10.clone.1 | convolution fusion | flops 281542656 | bytes 2261505 | tf_op jit(solution)/shard_map/while/body/eval_jaxpr/dot_general | solution.py:20
  126.3 17.5 %convolution_add_fusion.2 = f32[2048,128]{1,0:T(8,128)S(1)} fusion(f32[512]{0:T(512)S(1)} %bitcast.85, f32[2048]{0:T(1024)S(1)} %bitcast.77, f32[512]{0:T(512)S(1)} %bitcast.84, f32[2048]{0:T(1024)S(1)} %bitcast.78, f32[512]{0:T(512)S(1)} %bitcast.83, f32[2048]{0:T(1024)S(1)} %bitcast.76, f32[512]{0:T(512)S(1)} %bitcast.89, ...), kind=kOutput, calls=%fused_computation.10.clone.1 | convolution fusion | flops 281542656 | bytes 2261505 | tf_op jit(solution)/shard_map/while/body/eval_jaxpr/dot_general | solution.py:20
  145.5 17.5 %convolution_add_fusion.2 = f32[2048,128]{1,0:T(8,128)S(1)} fusion(f32[512]{0:T(512)S(1)} %bitcast.85, f32[2048]{0:T(1024)S(1)} %bitcast.77, f32[512]{0:T(512)S(1)} %bitcast.84, f32[2048]{0:T(1024)S(1)} %bitcast.78, f32[512]{0:T(512)S(1)} %bitcast.83, f32[2048]{0:T(1024)S(1)} %bitcast.76, f32[512]{0:T(512)S(1)} %bitcast.89, ...), kind=kOutput, calls=%fused_computation.10.clone.1 | convolution fusion | flops 281542656 | bytes 2261505 | tf_op jit(solution)/shard_map/while/body/eval_jaxpr/dot_general | solution.py:20
  164.3 120.4 %all-reduce.3.cloned.1.call-done = f32[2048,128]{1,0:T(8,128)} async-done(((f32[2048,128]{1,0:T(8,128)}), f32[2048,128]{1,0:T(8,128)}) %all-reduce.3.cloned.1.call-update) | async-done | bytes 1048592 | tf_op jit(solution)/shard_map/psum | solution.py:68
  284.7 4.1 fusion.22
  288.9 155.6 %all-reduce.5.cloned.1.call-done = f32[128,128]{0,1:T(8,128)} async-done(((f32[128,128]{0,1:T(8,128)}), f32[128,128]{0,1:T(8,128)}) %all-reduce.5.cloned.1.call-update) | async-done | bytes 65552 | tf_op jit(solution)/shard_map/psum | solution.py:69
  446.3 11.7 %cholesky.16 = f32[128,128]{1,0:T(8,128)S(1)} custom-call(f32[128,128]{1,0:T(8,128)S(1)} %fusion.18), custom_call_target="Cholesky" | custom-call | tf_op jit(solution)/shard_map/jit(cholesky)/cholesky | solution.py:35
  459.3 9.8 %custom-call.6 = f32[1,128,128]{1,2,0:T(8,128)S(1)} custom-call(f32[1,128,128]{2,1,0:T(8,128)S(1)} %fusion.15), custom_call_target="InvertDiagBlocksLowerTriangular" | custom-call | tf_op jit(solution)/shard_map/triangular_solve | solution.py:36
  471.1 144.9 %while.21 = (s32[]{:T(128)}, f32[8,512,128]{2,1,0:T(8,128)}, f32[8,512]{1,0:T(8,128)S(1)}, f32[3,2048]{1,0:T(4,128)S(1)}, f32[8,3,512]{2,1,0:T(4,128)}, /*index=...) while((s32[]{:T(128)}, f32[8,512,128]{2,1,0:T(8,128)}, f32[8,512]{1,0:T(8,128)S(1)}, ...), condition=%wide.region_7.8_spmd, body=%wide.region_6.7_spmd.sunk | while | flops 281018880 | bytes 885389 | solution.py:84
  472.0 17.3 %fusion.34 = f32[8,512,128]{2,1,0:T(8,128)} fusion(f32[8,512,128]{2,1,0:T(8,128)} %get-tuple-element.266, s32[]{:T(128)} %get-tuple-element.265, bf16[2048,128]{1,0:T(8,128)(2,1)S(1)} %get-tuple-element.280, f32[512]{0:T(512)S(1)} %bitcast.88, f32[2048]{0:T(1024)S(1)} %bitcast.80, f32[512]{0:T(512)S(1)} %bitcast.87, f32[2048]{0:T(1024)S(1)} %bitcast.81, ...), kind=kOutput, calls=%fused_computation.3.clone.1 | convolution fusion | flops 281018368 | bytes 819712 | tf_op jit(solution)/shard_map/while/body/eval_jaxpr/dot_general | solution.py:81
  490.1 17.3 %fusion.34 = f32[8,512,128]{2,1,0:T(8,128)} fusion(f32[8,512,128]{2,1,0:T(8,128)} %get-tuple-element.266, s32[]{:T(128)} %get-tuple-element.265, bf16[2048,128]{1,0:T(8,128)(2,1)S(1)} %get-tuple-element.280, f32[512]{0:T(512)S(1)} %bitcast.88, f32[2048]{0:T(1024)S(1)} %bitcast.80, f32[512]{0:T(512)S(1)} %bitcast.87, f32[2048]{0:T(1024)S(1)} %bitcast.81, ...), kind=kOutput, calls=%fused_computation.3.clone.1 | convolution fusion | flops 281018368 | bytes 819712 | tf_op jit(solution)/shard_map/while/body/eval_jaxpr/dot_general | solution.py:81
  508.2 17.3 %fusion.34 = f32[8,512,128]{2,1,0:T(8,128)} fusion(f32[8,512,128]{2,1,0:T(8,128)} %get-tuple-element.266, s32[]{:T(128)} %get-tuple-element.265, bf16[2048,128]{1,0:T(8,128)(2,1)S(1)} %get-tuple-element.280, f32[512]{0:T(512)S(1)} %bitcast.88, f32[2048]{0:T(1024)S(1)} %bitcast.80, f32[512]{0:T(512)S(1)} %bitcast.87, f32[2048]{0:T(1024)S(1)} %bitcast.81, ...), kind=kOutput, calls=%fused_computation.3.clone.1 | convolution fusion | flops 281018368 | bytes 819712 | tf_op jit(solution)/shard_map/while/body/eval_jaxpr/dot_general | solution.py:81
  526.3 17.3 %fusion.34 = f32[8,512,128]{2,1,0:T(8,128)} fusion(f32[8,512,128]{2,1,0:T(8,128)} %get-tuple-element.266, s32[]{:T(128)} %get-tuple-element.265, bf16[2048,128]{1,0:T(8,128)(2,1)S(1)} %get-tuple-element.280, f32[512]{0:T(512)S(1)} %bitcast.88, f32[2048]{0:T(1024)S(1)} %bitcast.80, f32[512]{0:T(512)S(1)} %bitcast.87, f32[2048]{0:T(1024)S(1)} %bitcast.81, ...), kind=kOutput, calls=%fused_computation.3.clone.1 | convolution fusion | flops 281018368 | bytes 819712 | tf_op jit(solution)/shard_map/while/body/eval_jaxpr/dot_general | solution.py:81
  544.4 17.2 %fusion.34 = f32[8,512,128]{2,1,0:T(8,128)} fusion(f32[8,512,128]{2,1,0:T(8,128)} %get-tuple-element.266, s32[]{:T(128)} %get-tuple-element.265, bf16[2048,128]{1,0:T(8,128)(2,1)S(1)} %get-tuple-element.280, f32[512]{0:T(512)S(1)} %bitcast.88, f32[2048]{0:T(1024)S(1)} %bitcast.80, f32[512]{0:T(512)S(1)} %bitcast.87, f32[2048]{0:T(1024)S(1)} %bitcast.81, ...), kind=kOutput, calls=%fused_computation.3.clone.1 | convolution fusion | flops 281018368 | bytes 819712 | tf_op jit(solution)/shard_map/while/body/eval_jaxpr/dot_general | solution.py:81
  562.5 17.2 %fusion.34 = f32[8,512,128]{2,1,0:T(8,128)} fusion(f32[8,512,128]{2,1,0:T(8,128)} %get-tuple-element.266, s32[]{:T(128)} %get-tuple-element.265, bf16[2048,128]{1,0:T(8,128)(2,1)S(1)} %get-tuple-element.280, f32[512]{0:T(512)S(1)} %bitcast.88, f32[2048]{0:T(1024)S(1)} %bitcast.80, f32[512]{0:T(512)S(1)} %bitcast.87, f32[2048]{0:T(1024)S(1)} %bitcast.81, ...), kind=kOutput, calls=%fused_computation.3.clone.1 | convolution fusion | flops 281018368 | bytes 819712 | tf_op jit(solution)/shard_map/while/body/eval_jaxpr/dot_general | solution.py:81
  580.6 17.2 %fusion.34 = f32[8,512,128]{2,1,0:T(8,128)} fusion(f32[8,512,128]{2,1,0:T(8,128)} %get-tuple-element.266, s32[]{:T(128)} %get-tuple-element.265, bf16[2048,128]{1,0:T(8,128)(2,1)S(1)} %get-tuple-element.280, f32[512]{0:T(512)S(1)} %bitcast.88, f32[2048]{0:T(1024)S(1)} %bitcast.80, f32[512]{0:T(512)S(1)} %bitcast.87, f32[2048]{0:T(1024)S(1)} %bitcast.81, ...), kind=kOutput, calls=%fused_computation.3.clone.1 | convolution fusion | flops 281018368 | bytes 819712 | tf_op jit(solution)/shard_map/while/body/eval_jaxpr/dot_general | solution.py:81
  598.7 17.3 %fusion.34 = f32[8,512,128]{2,1,0:T(8,128)} fusion(f32[8,512,128]{2,1,0:T(8,128)} %get-tuple-element.266, s32[]{:T(128)} %get-tuple-element.265, bf16[2048,128]{1,0:T(8,128)(2,1)S(1)} %get-tuple-element.280, f32[512]{0:T(512)S(1)} %bitcast.88, f32[2048]{0:T(1024)S(1)} %bitcast.80, f32[512]{0:T(512)S(1)} %bitcast.87, f32[2048]{0:T(1024)S(1)} %bitcast.81, ...), kind=kOutput, calls=%fused_computation.3.clone.1 | convolution fusion | flops 281018368 | bytes 819712 | tf_op jit(solution)/shard_map/while/body/eval_jaxpr/dot_general | solution.py:81
  616.0 222.9 %reduce-scatter.2.cloned.1.call-done = f32[128,128]{1,0:T(8,128)} async-done(((f32[4096,128]{1,0:T(8,128)}), f32[128,128]{1,0:T(8,128)}) %reduce-scatter.2.cloned.1.call-update) | async-done | bytes 65552 | tf_op jit(solution)/shard_map/reduce_scatter | solution.py:83
  (72 shorter events, 28.3 us)
Async XLA Ops:
  7.2 277.5 %all-reduce.3.cloned.1.call-start = ((), (), s32[]{:S(2)}) async-start(), calls=%async_computation.1 | async-start | bytes 2097152 | tf_op jit(solution)/shard_map/psum | solution.py:68
  163.3 1.0 copy-start.2
  164.3 280.2 %all-reduce.5.cloned.1.call-start = ((), (), s32[]{:S(2)}) async-start(), calls=%async_computation.2 | async-start | bytes 131072 | tf_op jit(solution)/shard_map/psum | solution.py:69
  284.7 184.5 %copy-start = (f32[2048,128]{1,0:T(8,128)S(1)}, f32[2048,128]{1,0:T(8,128)}, u32[]{:S(2)}) copy-start(f32[2048,128]{1,0:T(8,128)} %all-reduce.3.cloned.1.call-done) | copy-start | bytes 3145732
  288.8 182.3 %copy-start.1 = (f32[3,2048]{1,0:T(4,128)S(1)}, f32[3,2048]{1,0:T(4,128)}, u32[]{:S(2)}) copy-start(f32[3,2048]{1,0:T(4,128)} %get-tuple-element.291) | copy-start | bytes 73732
  288.8 550.0 %reduce-scatter.2.cloned.1.call-start = ((), (), s32[]{:S(2)}) async-start(), calls=%async_computation.3 | async-start | bytes 2162688 | tf_op jit(solution)/shard_map/reduce_scatter | solution.py:83
Sparse Core Ops, SparseCore 0:
  164.4 120.2 all-reduce.2
  289.0 155.4 all-reduce.4
  616.1 222.6 reduce-scatter.1
where the time goes:
time: 847 us; the launch traced here: 845 us
  waiting for transfers between devices  499 us (59%)
  matrix products  284 us (34%)
  other arithmetic  38.3 us (5%)
  between operations  13.8 us (2%)
  local copies, waits for them, and re-layouts  9.44 us (1%)
    reduce_scatter x1, waiting for transfers between devices, shards(): lax.psum_scatter(lax.map(project_block, (sub_src_blocks, sub_wts_blocks))...  223 us
    psum x1, waiting for transfers between devices, shards(): gram_matrix = lax.psum(gram_of(sketch), 'rows')  156 us
    dot_general x8, matrix products, contract_first(): lax.dot_general(left, right, (((0,), (0,)), ((), ())), preferred_element_...  140 us
    dot_general x8, matrix products, project_block(): return jnp.dot(kernel_tile, ortho_low, preferred_element_type=jnp.float32)  138 us
    psum x1, waiting for transfers between devices, shards(): sketch = lax.psum(partial_sketch, 'cols')  120 us
  transfers between devices with their start and end apart: 3, of which 3 were waited for; matrix products, arithmetic and copies ran while one was open for 0% of the time, Pallas kernels for 0%

commit v1 on v0

--- a/solution.py
+++ b/solution.py
@@ -66,7 +66,7 @@
         (src_blocks, wts_blocks, omega_blocks),
     )
     sketch = lax.psum(partial_sketch, "cols")
-    gram_matrix = lax.psum(gram_of(sketch), "rows")
+    gram_matrix = jnp.sum(lax.all_gather(gram_of(sketch), "rows"), axis=0)
     ortho = solve_rows(sketch, gram_matrix)
     ortho_low = ortho.astype(jnp.bfloat16)
     row_devices = lax.axis_size("rows")

time: 847 us -> 777 us (0.917)
  waiting for transfers between devices: 499 us -> 429 us
    psum x1 -> x0, waiting for transfers between devices: 156 us -> none  [shards(): gram_matrix = lax.psum(gram_of(sketch), 'rows')]
    all_gather x0 -> x1, waiting for transfers between devices: none -> 86.6 us  [shards(): gram_matrix = jnp.sum(lax.all_gather(gram_of(sketch), 'rows'), axis=0)]
where the time goes in v1:
time: 777 us; the launch traced here: 775 us
  waiting for transfers between devices  429 us (55%)
  matrix products  284 us (37%)
  other arithmetic  39.2 us (5%)
  between operations  13.8 us (2%)
  local copies, waits for them, and re-layouts  8.6 us (1%)
    reduce_scatter x1, waiting for transfers between devices, shards(): lax.psum_scatter(lax.map(project_block, (sub_src_blocks, sub_wts_blocks))...  222 us
    dot_general x8, matrix products, contract_first(): lax.dot_general(left, right, (((0,), (0,)), ((), ())), preferred_element_...  140 us
    dot_general x8, matrix products, project_block(): return jnp.dot(kernel_tile, ortho_low, preferred_element_type=jnp.float32)  138 us
    psum x1, waiting for transfers between devices, shards(): sketch = lax.psum(partial_sketch, 'cols')  120 us
    all_gather x1, waiting for transfers between devices, shards(): gram_matrix = jnp.sum(lax.all_gather(gram_of(sketch), 'rows'), axis=0)  86.6 us
  transfers between devices with their start and end apart: 3, of which 3 were waited for; matrix products, arithmetic and copies ran while one was open for 0% of the time, Pallas kernels for 0%

profile of v1, /device:TPU:8, one launch (start us, length us, event | category | flops | bytes accessed | tf_op | source)
XLA Modules:
  0.0 775.1 jit_solution(13377066195806939925)
XLA Ops:
  8.9 154.4 %while.22 = (s32[]{:T(128)}, f32[2048,128]{1,0:T(8,128)S(1)}, f32[8,512]{1,0:T(8,128)S(1)}, f32[3,2048]{1,0:T(4,128)}, f32[8,3,512]{2,1,0:T(4,128)}, /*index=5*/...) while((s32[]{:T(128)}, f32[2048,128]{1,0:T(8,128)S(1)}, f32[8,512]{1,0:T(8,128)S(1)}, ...), condition=%wide.region_1.2_spmd.clone, body=%wide.region_0.1_spmd.clone.sunk | while | flops 281543168 | bytes 2327191 | solution.py:63
  10.6 17.5 %convolution_add_fusion.2 = f32[2048,128]{1,0:T(8,128)S(1)} fusion(f32[512]{0:T(512)S(1)} %bitcast.87, f32[2048]{0:T(1024)S(1)} %bitcast.79, f32[512]{0:T(512)S(1)} %bitcast.86, f32[2048]{0:T(1024)S(1)} %bitcast.80, f32[512]{0:T(512)S(1)} %bitcast.85, f32[2048]{0:T(1024)S(1)} %bitcast.78, f32[512]{0:T(512)S(1)} %bitcast.91, ...), kind=kOutput, calls=%fused_computation.10.clone.1 | convolution fusion | flops 281542656 | bytes 2261505 | tf_op jit(solution)/shard_map/while/body/eval_jaxpr/dot_general | solution.py:20
  29.9 17.5 %convolution_add_fusion.2 = f32[2048,128]{1,0:T(8,128)S(1)} fusion(f32[512]{0:T(512)S(1)} %bitcast.87, f32[2048]{0:T(1024)S(1)} %bitcast.79, f32[512]{0:T(512)S(1)} %bitcast.86, f32[2048]{0:T(1024)S(1)} %bitcast.80, f32[512]{0:T(512)S(1)} %bitcast.85, f32[2048]{0:T(1024)S(1)} %bitcast.78, f32[512]{0:T(512)S(1)} %bitcast.91, ...), kind=kOutput, calls=%fused_computation.10.clone.1 | convolution fusion | flops 281542656 | bytes 2261505 | tf_op jit(solution)/shard_map/while/body/eval_jaxpr/dot_general | solution.py:20
  49.1 17.5 %convolution_add_fusion.2 = f32[2048,128]{1,0:T(8,128)S(1)} fusion(f32[512]{0:T(512)S(1)} %bitcast.87, f32[2048]{0:T(1024)S(1)} %bitcast.79, f32[512]{0:T(512)S(1)} %bitcast.86, f32[2048]{0:T(1024)S(1)} %bitcast.80, f32[512]{0:T(512)S(1)} %bitcast.85, f32[2048]{0:T(1024)S(1)} %bitcast.78, f32[512]{0:T(512)S(1)} %bitcast.91, ...), kind=kOutput, calls=%fused_computation.10.clone.1 | convolution fusion | flops 281542656 | bytes 2261505 | tf_op jit(solution)/shard_map/while/body/eval_jaxpr/dot_general | solution.py:20
  68.4 17.5 %convolution_add_fusion.2 = f32[2048,128]{1,0:T(8,128)S(1)} fusion(f32[512]{0:T(512)S(1)} %bitcast.87, f32[2048]{0:T(1024)S(1)} %bitcast.79, f32[512]{0:T(512)S(1)} %bitcast.86, f32[2048]{0:T(1024)S(1)} %bitcast.80, f32[512]{0:T(512)S(1)} %bitcast.85, f32[2048]{0:T(1024)S(1)} %bitcast.78, f32[512]{0:T(512)S(1)} %bitcast.91, ...), kind=kOutput, calls=%fused_computation.10.clone.1 | convolution fusion | flops 281542656 | bytes 2261505 | tf_op jit(solution)/shard_map/while/body/eval_jaxpr/dot_general | solution.py:20
  87.7 17.5 %convolution_add_fusion.2 = f32[2048,128]{1,0:T(8,128)S(1)} fusion(f32[512]{0:T(512)S(1)} %bitcast.87, f32[2048]{0:T(1024)S(1)} %bitcast.79, f32[512]{0:T(512)S(1)} %bitcast.86, f32[2048]{0:T(1024)S(1)} %bitcast.80, f32[512]{0:T(512)S(1)} %bitcast.85, f32[2048]{0:T(1024)S(1)} %bitcast.78, f32[512]{0:T(512)S(1)} %bitcast.91, ...), kind=kOutput, calls=%fused_computation.10.clone.1 | convolution fusion | flops 281542656 | bytes 2261505 | tf_op jit(solution)/shard_map/while/body/eval_jaxpr/dot_general | solution.py:20
  107.0 17.5 %convolution_add_fusion.2 = f32[2048,128]{1,0:T(8,128)S(1)} fusion(f32[512]{0:T(512)S(1)} %bitcast.87, f32[2048]{0:T(1024)S(1)} %bitcast.79, f32[512]{0:T(512)S(1)} %bitcast.86, f32[2048]{0:T(1024)S(1)} %bitcast.80, f32[512]{0:T(512)S(1)} %bitcast.85, f32[2048]{0:T(1024)S(1)} %bitcast.78, f32[512]{0:T(512)S(1)} %bitcast.91, ...), kind=kOutput, calls=%fused_computation.10.clone.1 | convolution fusion | flops 281542656 | bytes 2261505 | tf_op jit(solution)/shard_map/while/body/eval_jaxpr/dot_general | solution.py:20
  126.3 17.5 %convolution_add_fusion.2 = f32[2048,128]{1,0:T(8,128)S(1)} fusion(f32[512]{0:T(512)S(1)} %bitcast.87, f32[2048]{0:T(1024)S(1)} %bitcast.79, f32[512]{0:T(512)S(1)} %bitcast.86, f32[2048]{0:T(1024)S(1)} %bitcast.80, f32[512]{0:T(512)S(1)} %bitcast.85, f32[2048]{0:T(1024)S(1)} %bitcast.78, f32[512]{0:T(512)S(1)} %bitcast.91, ...), kind=kOutput, calls=%fused_computation.10.clone.1 | convolution fusion | flops 281542656 | bytes 2261505 | tf_op jit(solution)/shard_map/while/body/eval_jaxpr/dot_general | solution.py:20
  145.5 17.5 %convolution_add_fusion.2 = f32[2048,128]{1,0:T(8,128)S(1)} fusion(f32[512]{0:T(512)S(1)} %bitcast.87, f32[2048]{0:T(1024)S(1)} %bitcast.79, f32[512]{0:T(512)S(1)} %bitcast.86, f32[2048]{0:T(1024)S(1)} %bitcast.80, f32[512]{0:T(512)S(1)} %bitcast.85, f32[2048]{0:T(1024)S(1)} %bitcast.78, f32[512]{0:T(512)S(1)} %bitcast.91, ...), kind=kOutput, calls=%fused_computation.10.clone.1 | convolution fusion | flops 281542656 | bytes 2261505 | tf_op jit(solution)/shard_map/while/body/eval_jaxpr/dot_general | solution.py:20
  164.3 120.4 %all-reduce.2.cloned.1.call-done = f32[2048,128]{1,0:T(8,128)} async-done(((f32[2048,128]{1,0:T(8,128)}), f32[2048,128]{1,0:T(8,128)}) %all-reduce.2.cloned.1.call-update) | async-done | bytes 1048592 | tf_op jit(solution)/shard_map/psum | solution.py:68
  284.7 4.1 fusion.22
  288.9 86.6 %all-gather.3.cloned.1.call-done = f32[4096,128]{1,0:T(8,128)} async-done(((f32[128,128]{1,0:T(8,128)}), f32[4096,128]{1,0:T(8,128)}) %all-gather.3.cloned.1.call-update) | async-done | bytes 2097168 | tf_op jit(solution)/shard_map/all_gather | solution.py:69
  377.3 11.7 %cholesky.16 = f32[128,128]{1,0:T(8,128)S(1)} custom-call(f32[128,128]{1,0:T(8,128)S(1)} %fusion.18), custom_call_target="Cholesky" | custom-call | tf_op jit(solution)/shard_map/jit(cholesky)/cholesky | solution.py:35
  390.4 9.8 %custom-call.6 = f32[1,128,128]{1,2,0:T(8,128)S(1)} custom-call(f32[1,128,128]{2,1,0:T(8,128)S(1)} %fusion.15), custom_call_target="InvertDiagBlocksLowerTriangular" | custom-call | tf_op jit(solution)/shard_map/triangular_solve | solution.py:36
  402.2 144.9 %while.21 = (s32[]{:T(128)}, f32[8,512,128]{2,1,0:T(8,128)}, f32[8,512]{1,0:T(8,128)S(1)}, f32[3,2048]{1,0:T(4,128)S(1)}, f32[8,3,512]{2,1,0:T(4,128)}, /*index=...) while((s32[]{:T(128)}, f32[8,512,128]{2,1,0:T(8,128)}, f32[8,512]{1,0:T(8,128)S(1)}, ...), condition=%wide.region_7.8_spmd, body=%wide.region_6.7_spmd.sunk | while | flops 281018880 | bytes 885389 | solution.py:84
  403.0 17.3 %fusion.34 = f32[8,512,128]{2,1,0:T(8,128)} fusion(f32[8,512,128]{2,1,0:T(8,128)} %get-tuple-element.266, s32[]{:T(128)} %get-tuple-element.265, bf16[2048,128]{1,0:T(8,128)(2,1)S(1)} %get-tuple-element.280, f32[512]{0:T(512)S(1)} %bitcast.90, f32[2048]{0:T(1024)S(1)} %bitcast.82, f32[512]{0:T(512)S(1)} %bitcast.89, f32[2048]{0:T(1024)S(1)} %bitcast.83, ...), kind=kOutput, calls=%fused_computation.3.clone.1 | convolution fusion | flops 281018368 | bytes 819712 | tf_op jit(solution)/shard_map/while/body/eval_jaxpr/dot_general | solution.py:81
  421.1 17.3 %fusion.34 = f32[8,512,128]{2,1,0:T(8,128)} fusion(f32[8,512,128]{2,1,0:T(8,128)} %get-tuple-element.266, s32[]{:T(128)} %get-tuple-element.265, bf16[2048,128]{1,0:T(8,128)(2,1)S(1)} %get-tuple-element.280, f32[512]{0:T(512)S(1)} %bitcast.90, f32[2048]{0:T(1024)S(1)} %bitcast.82, f32[512]{0:T(512)S(1)} %bitcast.89, f32[2048]{0:T(1024)S(1)} %bitcast.83, ...), kind=kOutput, calls=%fused_computation.3.clone.1 | convolution fusion | flops 281018368 | bytes 819712 | tf_op jit(solution)/shard_map/while/body/eval_jaxpr/dot_general | solution.py:81
  439.2 17.3 %fusion.34 = f32[8,512,128]{2,1,0:T(8,128)} fusion(f32[8,512,128]{2,1,0:T(8,128)} %get-tuple-element.266, s32[]{:T(128)} %get-tuple-element.265, bf16[2048,128]{1,0:T(8,128)(2,1)S(1)} %get-tuple-element.280, f32[512]{0:T(512)S(1)} %bitcast.90, f32[2048]{0:T(1024)S(1)} %bitcast.82, f32[512]{0:T(512)S(1)} %bitcast.89, f32[2048]{0:T(1024)S(1)} %bitcast.83, ...), kind=kOutput, calls=%fused_computation.3.clone.1 | convolution fusion | flops 281018368 | bytes 819712 | tf_op jit(solution)/shard_map/while/body/eval_jaxpr/dot_general | solution.py:81
  457.3 17.3 %fusion.34 = f32[8,512,128]{2,1,0:T(8,128)} fusion(f32[8,512,128]{2,1,0:T(8,128)} %get-tuple-element.266, s32[]{:T(128)} %get-tuple-element.265, bf16[2048,128]{1,0:T(8,128)(2,1)S(1)} %get-tuple-element.280, f32[512]{0:T(512)S(1)} %bitcast.90, f32[2048]{0:T(1024)S(1)} %bitcast.82, f32[512]{0:T(512)S(1)} %bitcast.89, f32[2048]{0:T(1024)S(1)} %bitcast.83, ...), kind=kOutput, calls=%fused_computation.3.clone.1 | convolution fusion | flops 281018368 | bytes 819712 | tf_op jit(solution)/shard_map/while/body/eval_jaxpr/dot_general | solution.py:81
  475.5 17.2 %fusion.34 = f32[8,512,128]{2,1,0:T(8,128)} fusion(f32[8,512,128]{2,1,0:T(8,128)} %get-tuple-element.266, s32[]{:T(128)} %get-tuple-element.265, bf16[2048,128]{1,0:T(8,128)(2,1)S(1)} %get-tuple-element.280, f32[512]{0:T(512)S(1)} %bitcast.90, f32[2048]{0:T(1024)S(1)} %bitcast.82, f32[512]{0:T(512)S(1)} %bitcast.89, f32[2048]{0:T(1024)S(1)} %bitcast.83, ...), kind=kOutput, calls=%fused_computation.3.clone.1 | convolution fusion | flops 281018368 | bytes 819712 | tf_op jit(solution)/shard_map/while/body/eval_jaxpr/dot_general | solution.py:81
  493.6 17.2 %fusion.34 = f32[8,512,128]{2,1,0:T(8,128)} fusion(f32[8,512,128]{2,1,0:T(8,128)} %get-tuple-element.266, s32[]{:T(128)} %get-tuple-element.265, bf16[2048,128]{1,0:T(8,128)(2,1)S(1)} %get-tuple-element.280, f32[512]{0:T(512)S(1)} %bitcast.90, f32[2048]{0:T(1024)S(1)} %bitcast.82, f32[512]{0:T(512)S(1)} %bitcast.89, f32[2048]{0:T(1024)S(1)} %bitcast.83, ...), kind=kOutput, calls=%fused_computation.3.clone.1 | convolution fusion | flops 281018368 | bytes 819712 | tf_op jit(solution)/shard_map/while/body/eval_jaxpr/dot_general | solution.py:81
  511.7 17.3 %fusion.34 = f32[8,512,128]{2,1,0:T(8,128)} fusion(f32[8,512,128]{2,1,0:T(8,128)} %get-tuple-element.266, s32[]{:T(128)} %get-tuple-element.265, bf16[2048,128]{1,0:T(8,128)(2,1)S(1)} %get-tuple-element.280, f32[512]{0:T(512)S(1)} %bitcast.90, f32[2048]{0:T(1024)S(1)} %bitcast.82, f32[512]{0:T(512)S(1)} %bitcast.89, f32[2048]{0:T(1024)S(1)} %bitcast.83, ...), kind=kOutput, calls=%fused_computation.3.clone.1 | convolution fusion | flops 281018368 | bytes 819712 | tf_op jit(solution)/shard_map/while/body/eval_jaxpr/dot_general | solution.py:81
  529.8 17.3 %fusion.34 = f32[8,512,128]{2,1,0:T(8,128)} fusion(f32[8,512,128]{2,1,0:T(8,128)} %get-tuple-element.266, s32[]{:T(128)} %get-tuple-element.265, bf16[2048,128]{1,0:T(8,128)(2,1)S(1)} %get-tuple-element.280, f32[512]{0:T(512)S(1)} %bitcast.90, f32[2048]{0:T(1024)S(1)} %bitcast.82, f32[512]{0:T(512)S(1)} %bitcast.89, f32[2048]{0:T(1024)S(1)} %bitcast.83, ...), kind=kOutput, calls=%fused_computation.3.clone.1 | convolution fusion | flops 281018368 | bytes 819712 | tf_op jit(solution)/shard_map/while/body/eval_jaxpr/dot_general | solution.py:81
  547.1 221.5 %reduce-scatter.2.cloned.1.call-done = f32[128,128]{1,0:T(8,128)} async-done(((f32[4096,128]{1,0:T(8,128)}), f32[128,128]{1,0:T(8,128)}) %reduce-scatter.2.cloned.1.call-update) | async-done | bytes 65552 | tf_op jit(solution)/shard_map/reduce_scatter | solution.py:83
  (73 shorter events, 28.4 us)
Async XLA Ops:
  7.2 277.5 %all-reduce.2.cloned.1.call-start = ((), (), s32[]{:S(2)}) async-start(), calls=%async_computation.1 | async-start | bytes 2097152 | tf_op jit(solution)/shard_map/psum | solution.py:68
  163.3 1.0 copy-start.2
  164.3 211.2 %all-gather.3.cloned.1.call-start = ((), (), s32[]{:S(2)}) async-start(), calls=%async_computation.3 | async-start | bytes 2162688 | tf_op jit(solution)/shard_map/all_gather | solution.py:69
  284.7 115.5 %copy-start = (f32[2048,128]{1,0:T(8,128)S(1)}, f32[2048,128]{1,0:T(8,128)}, u32[]{:S(2)}) copy-start(f32[2048,128]{1,0:T(8,128)} %all-reduce.2.cloned.1.call-done) | copy-start | bytes 3145732
  288.8 479.8 %reduce-scatter.2.cloned.1.call-start = ((), (), s32[]{:S(2)}) async-start(), calls=%async_computation.2 | async-start | bytes 2162688 | tf_op jit(solution)/shard_map/reduce_scatter | solution.py:83
  377.2 24.9 %copy-start.1 = (f32[3,2048]{1,0:T(4,128)S(1)}, f32[3,2048]{1,0:T(4,128)}, u32[]{:S(2)}) copy-start(f32[3,2048]{1,0:T(4,128)} %get-tuple-element.292) | copy-start | bytes 73732
Sparse Core Ops, SparseCore 0:
  164.4 120.2 all-reduce.1
  288.9 86.5 all-gather.2
  547.2 221.3 reduce-scatter.1
